TPU v7x, 512 devices: a whole 4x8x8 slice. The times are simulated.
512 devices in a mesh: stn: 128 (over z, y, core), sec: 4 (over x).
Axes of the slice: x: 4, y: 8, z: 8, core: 2. Of those that a mesh axis runs over, the one named last changes fastest.
Arguments:
- voltages: bfloat16 [2, 128, 4, 2, 79872], P(None, 'stn', 'sec'), may hold values from -60 to 60
- bandpass: float32 [4, 6144], P('sec'), may hold values from 0.3 to 3
- station_flags: int32 [128], P('stn'), may hold values 0 or 1
- delays: int32 [256, 128], replicated, may hold values from 0 to 4095
- section: int32 [4], replicated, may hold values from 0 to 1, as said below
Outputs:
- visibilities: bfloat16 [4, 512, 256, 256], P('sec', 'stn')
- tied_beams: bfloat16 [4, 6144, 2, 2, 6, 256], P('sec', 'stn')
Inputs may be any that keep to these rules, and one draw needn't show every extreme that they name: Exactly 1 coarse channels have section 1, the others 0.
All inputs are finite; a program needn't handle non-finite values. No bound on the sum of `station_flags` on one device may be relied on, other than what follows from the above.
Results may differ from a plain program's by a relative error of at most 0.0055.
Values may be sent and summed in bfloat16 or wider, within the bound.
A program may use at most 64 MiB of HBM per device.

v0:
```python
import functools
import math

import jax
import jax.numpy as jnp
import numpy as np
from jax import lax
from jax.experimental import pallas as pl
from jax.experimental.pallas import tpu as pltpu
from jax.sharding import PartitionSpec as P

POLS = 2
NCH = 6144
TAPS = 8
FRAMES = 6
AVG = 12
BEAMS = 256
STATIONS = 128
INPUTS = STATIONS * POLS
PER_GROUP = 48
VIS_LOCAL = PER_GROUP // AVG
BLOCK = AVG * 2 * FRAMES
PERIOD = 65536
GAIN_LANE = 64
W_CHUNKS = 8
W_STEP = PER_GROUP // W_CHUNKS
PLANES = 8
PLANE = STATIONS // PLANES
SECTIONS = 4
MESH = pl.DeviceIdType.MESH

NT = (((1,), (1,)), ((), ()))
NN = (((1,), (0,)), ((), ()))


def dot_f32(lhs, rhs, dims):
    return lax.dot_general(lhs, rhs, dims, preferred_element_type=jnp.float32)


def swap_table():
    table = np.zeros((VIS_LOCAL, INPUTS, INPUTS), np.float32)
    for v in range(VIS_LOCAL):
        for q in range(BLOCK):
            real = q % 12 < 6
            table[v, 16 * v + q, 16 * v + (q + 6 if real else q - 6)] = -1.0 if real else 1.0
    return table


def split_table():
    table = np.zeros((INPUTS, INPUTS), np.float32)
    for pol in range(POLS):
        for station in range(STATIONS):
            table[pol * STATIONS + station, station * POLS + pol] = 1.0
    return table


def finish_kernel(
    section_ref,
    w_hbm_ref,
    r_ref,
    swap_ref,
    split_ref,
    vis_ref,
    beam_ref,
    xl_ref,
    xs_ref,
    w_ref,
    w_sem,
):
    is_beam = section_ref[lax.axis_index("sec")] == 1

    @pl.when(jnp.logical_not(is_beam))
    def _():
        beam_ref[...] = jnp.zeros_like(beam_ref)
        last = r_ref[VIS_LOCAL]
        gain_col = jnp.sum(
            last[:, GAIN_LANE : GAIN_LANE + 3].astype(jnp.float32), axis=1, keepdims=True
        )
        gain_col = gain_col * (1.0 / math.sqrt(FRAMES * AVG))
        lane8 = lax.broadcasted_iota(jnp.int32, (8, 128), 1)
        pick = jnp.where((lane8 >= GAIN_LANE) & (lane8 < GAIN_LANE + 3), 1.0, 0.0)
        gain_row = dot_f32(pick.astype(jnp.bfloat16), last, NT)[0:1, :]
        rows = lax.broadcasted_iota(jnp.int32, (INPUTS, INPUTS), 0)
        cols = lax.broadcasted_iota(jnp.int32, (INPUTS, INPUTS), 1)
        for v in range(VIS_LOCAL):
            left = jnp.concatenate([r_ref[v], r_ref[v + 1]], axis=1)
            inside = (cols >= 16 * v) & (cols < 16 * v + BLOCK)
            same = jnp.where(inside, left.astype(jnp.float32), 0.0).astype(jnp.bfloat16)
            other = dot_f32(left, swap_ref[v], NT).astype(jnp.bfloat16)
            real = dot_f32(left, same, NT)
            imag = dot_f32(left, other, NT)
            packed = jnp.where(rows <= cols, real, imag)
            vis_ref[v] = (packed * gain_col * gain_row).astype(jnp.bfloat16)

    @pl.when(is_beam)
    def _():
        copies = []
        for n in range(W_CHUNKS):
            part = pl.ds(W_STEP * n, W_STEP)
            copies.append(
                pltpu.make_async_copy(w_hbm_ref.at[part], w_ref.at[part], w_sem.at[n])
            )
            copies[n].start()
        vis_ref[...] = jnp.zeros_like(vis_ref)
        gain = None
        for j in range(VIS_LOCAL, -1, -1):
            part = dot_f32(split_ref[...], r_ref[j], NN)
            if gain is None:
                gain = jnp.sum(part[:, GAIN_LANE : GAIN_LANE + 3], axis=1, keepdims=True)
            xs_ref[j] = (part * gain).astype(jnp.bfloat16)
        q_row = lax.broadcasted_iota(jnp.int32, (BLOCK, INPUTS), 0)
        q_col = lax.broadcasted_iota(jnp.int32, (BLOCK, INPUTS), 1)
        for v in range(VIS_LOCAL):
            window = jnp.concatenate([xs_ref[v], xs_ref[v + 1]], axis=1)
            keep = jnp.where(q_col == q_row + 16 * v, 1.0, 0.0).astype(jnp.bfloat16)
            plain = dot_f32(keep, window, NT)
            other = dot_f32(swap_ref[v, 16 * v : 16 * v + BLOCK, :], window, NT)
            for pol in range(POLS):
                rows = pl.ds(2 * BLOCK * v + pol, BLOCK, stride=2)
                half = slice(128 * pol, 128 * pol + 128)
                xl_ref[0, rows, :] = plain[:, half]
                xl_ref[1, rows, :] = other[:, half]
        scale = 1.0 / math.sqrt(STATIONS)

        def one_channel(k, carry):
            rows = pl.ds(pl.multiple_of(24 * k, 8), 24)
            left = jnp.concatenate([xl_ref[0, rows, :], xl_ref[1, rows, :]], axis=1)
            out = dot_f32(left.astype(jnp.bfloat16), w_ref[k], NN) * scale
            beam_ref[k] = out.astype(jnp.bfloat16).reshape(2 * FRAMES, POLS, BEAMS)
            return carry

        for n in range(W_CHUNKS):
            copies[n].wait()
            lax.fori_loop(W_STEP * n, W_STEP * (n + 1), one_channel, 0, unroll=3)


def finish(section, weights, received):
    vmem = pl.BlockSpec(memory_space=pltpu.VMEM)
    vis, beam = pl.pallas_call(
        finish_kernel,
        out_shape=(
            jax.ShapeDtypeStruct((VIS_LOCAL, INPUTS, INPUTS), jnp.bfloat16),
            jax.ShapeDtypeStruct((PER_GROUP, 2 * FRAMES, POLS, BEAMS), jnp.bfloat16),
        ),
        in_specs=[
            pl.BlockSpec(memory_space=pltpu.SMEM),
            pl.BlockSpec(memory_space=pl.ANY),
            vmem,
            vmem,
            vmem,
        ],
        out_specs=(vmem, vmem),
        scratch_shapes=[
            pltpu.VMEM((2, PER_GROUP * 24, 128), jnp.float32),
            pltpu.VMEM((5, INPUTS, 128), jnp.bfloat16),
            pltpu.VMEM((PER_GROUP, INPUTS, BEAMS), jnp.bfloat16),
            pltpu.SemaphoreType.DMA((W_CHUNKS,)),
        ],
        name="finish",
    )(
        section,
        weights,
        received,
        jnp.asarray(swap_table(), jnp.bfloat16),
        jnp.asarray(split_table(), jnp.bfloat16),
    )
    tied = beam.reshape(PER_GROUP, 2, FRAMES, POLS, BEAMS).transpose(0, 1, 3, 2, 4)
    return vis, tied


def split2(value):
    high = value.astype(jnp.bfloat16)
    return high, (value - high.astype(jnp.float32)).astype(jnp.bfloat16)


def split_const(table):
    table = np.asarray(table, np.float32)
    high = table.astype(jnp.bfloat16)
    return high, (table - high.astype(np.float32)).astype(jnp.bfloat16)


def taper_table():
    index = np.arange(TAPS * NCH, dtype=np.float64)
    offset = (index + 0.5 - TAPS * NCH / 2.0) / NCH
    window = 0.5 - 0.5 * np.cos(2.0 * np.pi * (index + 0.5) / (TAPS * NCH))
    table = (np.sinc(offset) * window).reshape(TAPS, PER_GROUP, 1, 128)
    table = np.broadcast_to(table, (TAPS, PER_GROUP, POLS, 128))
    return table.reshape(TAPS, 2 * PER_GROUP, 128).astype(np.float32)


def outer_table():
    angle = 2.0 * np.pi * (np.outer(np.arange(48), np.arange(48)) % 48) / 48.0
    cos, sin = np.cos(angle), np.sin(angle)
    table = np.zeros((POLS, 2, 48, 2, 48, POLS))
    for pol in range(POLS):
        table[pol, 0, :, 0, :, pol] = cos
        table[pol, 0, :, 1, :, pol] = sin
        table[pol, 1, :, 0, :, pol] = -sin
        table[pol, 1, :, 1, :, pol] = cos
    return table.reshape(192, 192)


def twist_tables():
    angle = 2.0 * np.pi * np.outer(np.arange(48), np.arange(128)) / NCH
    return np.stack([np.cos(angle), np.sin(angle)]).astype(np.float32)


def inner_table():
    angle = 2.0 * np.pi * (np.outer(np.arange(128), np.arange(128)) % 128) / 128.0
    return np.concatenate([np.cos(angle), np.sin(angle)], axis=1)


def spread_table():
    row, col = np.arange(384)[:, None], np.arange(640)[None, :]
    return ((row % 48 == col // 12) & (col < 576)).astype(np.float32)


def make_weights(delays, first, w_ref):
    delay = delays.astype(jnp.float32).T.astype(jnp.int32)
    turn = 2.0 * math.pi / PERIOD
    start = (delay * first & (PERIOD - 1)).astype(jnp.float32) * turn
    step = delay.astype(jnp.float32) * turn
    state = (jnp.cos(start), jnp.sin(start), jnp.cos(step), jnp.sin(step))
    for sb in range(8):
        cs, sn, dc, ds = (t[16 * sb : 16 * sb + 16] for t in state)

        def advance(k, carry):
            c, s = carry
            w_ref[k, 16 * sb : 16 * sb + 16, :] = c.astype(jnp.bfloat16)
            w_ref[k, 128 + 16 * sb : 128 + 16 * sb + 16, :] = s.astype(jnp.bfloat16)
            return (c * dc - s * ds, c * ds + s * dc)

        lax.fori_loop(0, PER_GROUP, advance, (cs, sn), unroll=4)


def channelize_kernel(
    flag_ref,
    volt_hbm,
    band_hbm,
    delays_hbm,
    taper_hbm,
    outer_h_hbm,
    outer_l_hbm,
    twist_hbm,
    inner_h_hbm,
    inner_l_hbm,
    spread_hbm,
    recv_ref,
    w_hbm,
    volt_ref,
    band_ref,
    delays_ref,
    taper_ref,
    outer_h_ref,
    outer_l_ref,
    twist_ref,
    inner_h_ref,
    inner_l_ref,
    spread_ref,
    fh_ref,
    fl_ref,
    y_ref,
    o_ref,
    send_ref,
    pow_ref,
    w_ref,
    load_sem,
    send_sem,
    recv_sem,
    own_sem,
    w_sem,
    ready_sem,
):
    me, sec = lax.axis_index("stn"), lax.axis_index("sec")
    plane, place = me // PLANE, lax.rem(me, PLANE)
    barrier = pltpu.get_barrier_semaphore()
    loads = [
        pltpu.make_async_copy(src, dst, load_sem.at[n])
        for n, (src, dst) in enumerate(
            (
                (volt_hbm, volt_ref),
                (taper_hbm, taper_ref),
                (band_hbm, band_ref),
                (spread_hbm, spread_ref),
                (outer_h_hbm, outer_h_ref),
                (outer_l_hbm, outer_l_ref),
                (twist_hbm, twist_ref),
                (inner_h_hbm, inner_h_ref),
                (inner_l_hbm, inner_l_ref),
                (delays_hbm, delays_ref),
            )
        )
    ]
    for load in loads:
        load.start()

    for i in range(1, PLANE):
        other = plane * PLANE + lax.rem(place + i, PLANE)
        pl.semaphore_signal(barrier, inc=1, device_id=(other, sec), device_id_type=MESH)
    for i in range(1, SECTIONS):
        other = lax.rem(sec + i, SECTIONS)
        pl.semaphore_signal(barrier, inc=1, device_id=(me, other), device_id_type=MESH)
    for load in loads[:-1]:
        load.wait()

    group = lax.broadcasted_iota(jnp.int32, (8, 128), 0)
    lane8 = lax.broadcasted_iota(jnp.int32, (8, 128), 1)
    spread_parts = []
    for q in range(3):
        inside = (lane8 + 128 * q >= 48 * group) & (lane8 + 128 * q < 48 * group + 48)
        tiles = [
            jnp.where(inside, band_ref[0:1, 384 * t + 128 * q : 384 * t + 128 * q + 128], 0.0)
            for t in range(16)
        ]
        spread_parts.append(jnp.concatenate(tiles, axis=0))
    band_h, band_l = split2(jnp.concatenate(spread_parts, axis=1))

    for part in range(2):
        for chunk in range(6):
            rows = slice(16 * chunk, 16 * chunk + 16)
            taps = [taper_ref[j, rows, :] for j in range(TAPS)]
            blocks = [
                volt_ref[part, 96 * n + 16 * chunk : 96 * n + 16 * chunk + 16, :].astype(jnp.float32)
                for n in range(FRAMES + TAPS - 1)
            ]
            for m in range(FRAMES):
                total = taps[0] * blocks[m]
                for j in range(1, TAPS):
                    total = total + taps[j] * blocks[m + j]
                high, low = split2(total)
                at = slice(96 * part + 16 * chunk, 96 * part + 16 * chunk + 16)
                fh_ref[at, 128 * m : 128 * m + 128] = high
                fl_ref[at, 128 * m : 128 * m + 128] = low

    cos, sin = twist_ref[0], twist_ref[1]
    for pair in range(FRAMES // 2):
        lanes = slice(256 * pair, 256 * pair + 256)
        fh = fh_ref[:, lanes]
        seg = dot_f32(outer_h_ref[...], fh, NN)
        seg = seg + dot_f32(outer_l_ref[...], fh, NN)
        seg = seg + dot_f32(outer_h_ref[...], fl_ref[:, lanes], NN)
        for half in range(2):
            m = 2 * pair + half
            for pol in range(POLS):
                sr = seg[96 * pol : 96 * pol + 48, 128 * half : 128 * half + 128]
                si = seg[96 * pol + 48 : 96 * pol + 96, 128 * half : 128 * half + 128]
                yr = sr * cos + si * sin
                yi = si * cos - sr * sin
                real_rows = pl.ds(m, 48, stride=12)
                imag_rows = pl.ds(FRAMES + m, 48, stride=12)
                y_ref[2 * pol, real_rows, :] = yr
                y_ref[2 * pol + 1, real_rows, :] = yi
                y_ref[2 * pol, imag_rows, :] = yi
                y_ref[2 * pol + 1, imag_rows, :] = -yr

    powers = [jnp.zeros((8, 128), jnp.float32) for _ in range(POLS)]
    for first, count in ((0, 2), (2, 2), (4, 1)):
        width = 128 * count
        depth = min(width, 576 - 128 * first)
        columns = spread_ref[:, 128 * first : 128 * first + width]
        spread = dot_f32(band_h, columns, NN) + dot_f32(band_l, columns, NN)
        for pol in range(POLS):
            y = jnp.concatenate(
                [y_ref[2 * pol + t, 128 * first : 128 * first + depth, :] for t in range(2)], axis=1
            )
            if depth < width:
                y = jnp.concatenate([y, jnp.zeros((width - depth, 256), jnp.float32)], axis=0)
            yh, yl = split2(y)
            out = dot_f32(inner_h_ref[...], yh, NT)
            out = out + dot_f32(inner_l_ref[...], yh, NT)
            out = out + dot_f32(inner_h_ref[...], yl, NT)
            out = out * spread
            square = out * out
            for t in range(count):
                piece = slice(128 * t, 128 * t + 128)
                o_ref[first + t, pl.ds(pol, 128, stride=2), :] = out[:, piece]
                powers[pol] = powers[pol] + jnp.sum(square[:, piece].reshape(16, 8, 128), axis=0)
    for j in range(4):
        send_ref[j] = o_ref[j].astype(jnp.bfloat16).reshape(128, 2, 128)
    lane = lax.broadcasted_iota(jnp.int32, (1, 128), 1)
    totals = [jnp.sum(p, keepdims=True) for p in powers]
    pow_ref[SECTIONS] = jnp.where(lane < 64, totals[0], totals[1])

    pl.semaphore_wait(barrier, PLANE - 1 + SECTIONS - 1 + plane)

    def greet_later(z, carry):
        pl.semaphore_signal(
            barrier, inc=1, device_id=(z * PLANE + place, sec), device_id_type=MESH
        )
        return carry

    def greet_earlier(z, carry):
        pl.semaphore_signal(
            ready_sem.at[plane], inc=1, device_id=(z * PLANE + place, sec), device_id_type=MESH
        )
        return carry

    lax.fori_loop(0, plane, greet_earlier, 0)
    lax.fori_loop(plane + 1, PLANES, greet_later, 0)

    def power_copy(j):
        return pltpu.make_async_remote_copy(
            src_ref=pow_ref.at[SECTIONS],
            dst_ref=pow_ref.at[sec],
            send_sem=send_sem.at[0],
            recv_sem=recv_sem.at[0],
            device_id=(me, lax.rem(sec + j, SECTIONS)),
            device_id_type=MESH,
        )

    for j in range(1, SECTIONS):
        power_copy(j).start()

    def block_copy(to, tiles):
        return pltpu.make_async_remote_copy(
            src_ref=send_ref.at[tiles, to],
            dst_ref=recv_ref.at[tiles, me],
            send_sem=send_sem.at[1],
            recv_sem=recv_sem.at[1],
            device_id=(to, sec),
            device_id_type=MESH,
        )

    body, tail, whole = pl.ds(0, 4), pl.ds(4, 1), pl.ds(0, 5)

    def send_plane(z, tiles, start):
        for i in range(start, PLANE):
            block_copy(z * PLANE + lax.rem(place + i, PLANE), tiles).start()

    def send_entered(tiles):
        def one(n, carry):
            odd = lax.rem(n, 2)
            z = (1 - odd) * (n // 2) + odd * (plane - 1 - n // 2)
            send_plane(z, tiles, 0)
            return carry

        send_plane(plane, tiles, 1)
        lax.fori_loop(0, plane, one, 0)

    send_entered(body)

    def bytes_of(ref, slot):
        return pltpu.make_async_remote_copy(
            src_ref=ref,
            dst_ref=ref,
            send_sem=send_sem.at[slot],
            recv_sem=recv_sem.at[slot],
            device_id=(me, sec),
            device_id_type=MESH,
        )

    three = bytes_of(pow_ref.at[pl.ds(0, SECTIONS - 1)], 0)
    three.wait_send()
    three.wait_recv()
    mine = lax.broadcasted_iota(jnp.int32, (1, 128), 1) * 0 + sec
    total = pow_ref[SECTIONS]
    for other in range(SECTIONS):
        total = total + jnp.where(mine == other, 0.0, pow_ref[other])
    mean = total * (1.0 / (SECTIONS * FRAMES * NCH))
    gain = jnp.where(flag_ref[0] == 1, 0.0, 1.0 / jnp.sqrt(mean + 1e-05))
    g0 = gain.astype(jnp.bfloat16).astype(jnp.float32)
    g1 = (gain - g0).astype(jnp.bfloat16).astype(jnp.float32)
    g2 = gain - g0 - g1
    row = lax.broadcasted_iota(jnp.int32, (8, 128), 0)
    col = lax.broadcasted_iota(jnp.int32, (8, 128), 1)
    patch = jnp.zeros((8, 128), jnp.float32)
    for at, g in ((0, g0), (1, g1), (2, g2)):
        pair = jnp.where(row % 2 == 0, g[:, 0:1], g[:, 64:65])
        patch = jnp.where(col == GAIN_LANE + at, pair, patch)
    patch = jnp.broadcast_to(patch[None], (INPUTS // 8, 8, 128)).reshape(INPUTS, 128)
    wide = lax.broadcasted_iota(jnp.int32, (INPUTS, 128), 1)
    tile = jnp.where(wide < GAIN_LANE, o_ref[4], patch)
    send_ref[4] = tile.astype(jnp.bfloat16).reshape(128, 2, 128)
    send_entered(tail)

    def send_later(z, carry):
        pl.semaphore_wait(ready_sem.at[z], 1)
        send_plane(z, whole, 0)
        return carry

    lax.fori_loop(plane + 1, PLANES, send_later, 0)
    own = pltpu.make_async_copy(send_ref.at[:, me], recv_ref.at[:, me], own_sem)
    own.start()
    loads[-1].wait()
    make_weights(delays_ref[...], sec * NCH + me * PER_GROUP, w_ref)
    save = pltpu.make_async_copy(w_ref, w_hbm, w_sem)
    save.start()
    own.wait()
    sent = bytes_of(send_ref.at[:, pl.ds(0, STATIONS - 1)], 1)
    sent.wait_send()
    save.wait()
    landed = bytes_of(recv_ref.at[:, pl.ds(0, STATIONS - 1)], 1)
    landed.wait_recv()


def channelize(flags, volts, band, delays):
    outer_h, outer_l = split_const(outer_table())
    inner_h, inner_l = split_const(inner_table())
    operands = [
        volts,
        band,
        delays,
        jnp.asarray(taper_table()),
        jnp.asarray(outer_h),
        jnp.asarray(outer_l),
        jnp.asarray(twist_tables()),
        jnp.asarray(inner_h),
        jnp.asarray(inner_l),
        jnp.asarray(spread_table(), jnp.bfloat16),
    ]
    anywhere = pl.BlockSpec(memory_space=pl.ANY)
    return pl.pallas_call(
        channelize_kernel,
        out_shape=(
            jax.ShapeDtypeStruct((5, STATIONS, POLS, 128), jnp.bfloat16),
            jax.ShapeDtypeStruct((PER_GROUP, INPUTS, BEAMS), jnp.bfloat16),
        ),
        in_specs=[pl.BlockSpec(memory_space=pltpu.SMEM)] + [anywhere] * len(operands),
        out_specs=(anywhere, anywhere),
        scratch_shapes=[pltpu.VMEM(x.shape, x.dtype) for x in operands]
        + [
            pltpu.VMEM((192, 768), jnp.bfloat16),
            pltpu.VMEM((192, 768), jnp.bfloat16),
            pltpu.VMEM((4, 576, 128), jnp.float32),
            pltpu.VMEM((5, 256, 128), jnp.float32),
            pltpu.VMEM((5, STATIONS, POLS, 128), jnp.bfloat16),
            pltpu.VMEM((5, 1, 128), jnp.float32),
            pltpu.VMEM((PER_GROUP, INPUTS, BEAMS), jnp.bfloat16),
            pltpu.SemaphoreType.DMA((len(operands),)),
            pltpu.SemaphoreType.DMA((2,)),
            pltpu.SemaphoreType.DMA((2,)),
            pltpu.SemaphoreType.DMA,
            pltpu.SemaphoreType.DMA,
            pltpu.SemaphoreType.REGULAR((PLANES,)),
        ],
        compiler_params=pltpu.CompilerParams(collective_id=0, has_side_effects=True),
        name="channelize",
    )(flags, *operands)


def per_device(voltages, bandpass, station_flags, delays, section):
    volts = voltages.reshape(2, POLS, 624, 128).transpose(0, 2, 1, 3).reshape(2, 1248, 128)
    turned, weights = channelize(station_flags, volts, bandpass, delays)
    vis, tied = finish(section, weights, turned.reshape(5, INPUTS, 128))
    return (vis[None], tied[None])


def solution(mesh):
    return jax.shard_map(
        per_device,
        mesh=mesh,
        in_specs=(P(None, "stn", "sec", None, None), P("sec", None), P("stn"), P(), P()),
        out_specs=(P("sec", "stn", None, None), P("sec", "stn", None, None, None, None)),
        check_vma=False,
    )
```

profile of v0, /device:TPU:7, one launch (start us, length us, event | category | flops | bytes accessed | tf_op | source)
XLA Modules:
  0.0 34.6 jit_solution(3601747811526508541)
XLA Ops:
  1.3 26.7 %channelize.1 = (bf16[5,128,2,128]{3,2,1,0:T(2,128)(2,1)}, bf16[48,256,256]{2,1,0:T(8,128)(2,1)}) custom-call(s32[1]{0:T(128)S(6)} %copy.17.flag_ref, bf16[2,1248,128]{2,1,0:T(8,128)(2,1)} %bitcast.12, f32[1,6144]{1,0:T(1,128)} %band_hbm.1, s32[256,128]{1,0:T(8,128)} %delays_hbm.1, f32[8,96,128]{2,1,0:T(8,128)} %constant.18.clone.taper_hbm, ...), custom_call_target="tpu_custom_call" | custom-call | tf_op jit(solution)/shard_map/channelize/pallas_call | solution.py:512
  28.0 6.6 %finish.1 = (bf16[4,256,256]{2,1,0:T(8,128)(2,1)}, bf16[48,12,2,256]{3,2,1,0:T(2,128)(2,1)}) custom-call(s32[4]{0:T(128)} %section_ref.1, bf16[48,256,256]{2,1,0:T(8,128)(2,1)} %get-tuple-element.6.w_hbm_ref, bf16[5,256,128]{2,1,0:T(8,128)(2,1)} %bitcast.13, bf16[4,256,256]{2,1,0:T(8,128)(2,1)} %constant.25.clone.swap_ref, ...), custom_call_target="tpu_custom_call" | custom-call | tf_op jit(solution)/shard_map/finish/pallas_call | solution.py:139
where the time goes:
time: 34.8 us; the launch traced here: 34.6 us
  Pallas kernels  33.3 us (96%)
  between operations  1.28 us (4%)
    pallas_call x1, Pallas kernels, channelize(): pl.pallas_call(channelize_kernel, out_shape=(jax.ShapeDtypeStruct((5, STA...  26.7 us
    pallas_call x1, Pallas kernels, finish(): pl.pallas_call(finish_kernel, out_shape=(jax.ShapeDtypeStruct((VIS_LOCAL,...  6.62 us

commit v1 on v0

--- a/solution.py
+++ b/solution.py
@@ -22,8 +22,8 @@
 BLOCK = AVG * 2 * FRAMES
 PERIOD = 65536
 GAIN_LANE = 64
-W_CHUNKS = 8
-W_STEP = PER_GROUP // W_CHUNKS
+OUT_CHUNKS = 4
+OUT_STEP = PER_GROUP // OUT_CHUNKS
 PLANES = 8
 PLANE = STATIONS // PLANES
 SECTIONS = 4
@@ -56,22 +56,27 @@
 
 def finish_kernel(
     section_ref,
-    w_hbm_ref,
+    w_ref,
     r_ref,
     swap_ref,
     split_ref,
+    vis_hbm,
+    beam_hbm,
     vis_ref,
     beam_ref,
     xl_ref,
     xs_ref,
-    w_ref,
-    w_sem,
+    out_sem,
+    zero_sem,
 ):
-    is_beam = section_ref[lax.axis_index("sec")] == 1
+    is_beam = jnp.max(section_ref[...]) == 1.0
 
     @pl.when(jnp.logical_not(is_beam))
     def _():
         beam_ref[...] = jnp.zeros_like(beam_ref)
+        zero = pltpu.make_async_copy(beam_ref, beam_hbm, zero_sem)
+        zero.start()
+        copies = []
         last = r_ref[VIS_LOCAL]
         gain_col = jnp.sum(
             last[:, GAIN_LANE : GAIN_LANE + 3].astype(jnp.float32), axis=1, keepdims=True
@@ -91,17 +96,17 @@
             imag = dot_f32(left, other, NT)
             packed = jnp.where(rows <= cols, real, imag)
             vis_ref[v] = (packed * gain_col * gain_row).astype(jnp.bfloat16)
+            copies.append(pltpu.make_async_copy(vis_ref.at[v], vis_hbm.at[v], out_sem.at[v]))
+            copies[v].start()
+        for copy in copies:
+            copy.wait()
+        zero.wait()
 
     @pl.when(is_beam)
     def _():
-        copies = []
-        for n in range(W_CHUNKS):
-            part = pl.ds(W_STEP * n, W_STEP)
-            copies.append(
-                pltpu.make_async_copy(w_hbm_ref.at[part], w_ref.at[part], w_sem.at[n])
-            )
-            copies[n].start()
         vis_ref[...] = jnp.zeros_like(vis_ref)
+        zero = pltpu.make_async_copy(vis_ref, vis_hbm, zero_sem)
+        zero.start()
         gain = None
         for j in range(VIS_LOCAL, -1, -1):
             part = dot_f32(split_ref[...], r_ref[j], NN)
@@ -129,41 +134,43 @@
             beam_ref[k] = out.astype(jnp.bfloat16).reshape(2 * FRAMES, POLS, BEAMS)
             return carry
 
-        for n in range(W_CHUNKS):
-            copies[n].wait()
-            lax.fori_loop(W_STEP * n, W_STEP * (n + 1), one_channel, 0, unroll=3)
-
-
-def finish(section, weights, received):
+        copies = []
+        for n in range(OUT_CHUNKS):
+            lax.fori_loop(OUT_STEP * n, OUT_STEP * (n + 1), one_channel, 0, unroll=4)
+            part = pl.ds(OUT_STEP * n, OUT_STEP)
+            copies.append(
+                pltpu.make_async_copy(beam_ref.at[part], beam_hbm.at[part], out_sem.at[n])
+            )
+            copies[n].start()
+        for copy in copies:
+            copy.wait()
+        zero.wait()
+
+
+def finish(section, weights, received, swap, split):
     vmem = pl.BlockSpec(memory_space=pltpu.VMEM)
+    anywhere = pl.BlockSpec(memory_space=pl.ANY)
+    vis_shape = (VIS_LOCAL, INPUTS, INPUTS)
+    beam_shape = (PER_GROUP, 2 * FRAMES, POLS, BEAMS)
     vis, beam = pl.pallas_call(
         finish_kernel,
         out_shape=(
-            jax.ShapeDtypeStruct((VIS_LOCAL, INPUTS, INPUTS), jnp.bfloat16),
-            jax.ShapeDtypeStruct((PER_GROUP, 2 * FRAMES, POLS, BEAMS), jnp.bfloat16),
+            jax.ShapeDtypeStruct(vis_shape, jnp.bfloat16),
+            jax.ShapeDtypeStruct(beam_shape, jnp.bfloat16),
         ),
-        in_specs=[
-            pl.BlockSpec(memory_space=pltpu.SMEM),
-            pl.BlockSpec(memory_space=pl.ANY),
-            vmem,
-            vmem,
-            vmem,
-        ],
-        out_specs=(vmem, vmem),
+        in_specs=[vmem] * 5,
+        out_specs=(anywhere, anywhere),
         scratch_shapes=[
+            pltpu.VMEM(vis_shape, jnp.bfloat16),
+            pltpu.VMEM(beam_shape, jnp.bfloat16),
             pltpu.VMEM((2, PER_GROUP * 24, 128), jnp.float32),
             pltpu.VMEM((5, INPUTS, 128), jnp.bfloat16),
-            pltpu.VMEM((PER_GROUP, INPUTS, BEAMS), jnp.bfloat16),
-            pltpu.SemaphoreType.DMA((W_CHUNKS,)),
+            pltpu.SemaphoreType.DMA((4,)),
+            pltpu.SemaphoreType.DMA,
         ],
+        compiler_params=pltpu.CompilerParams(vmem_limit_bytes=24 << 20),
         name="finish",
-    )(
-        section,
-        weights,
-        received,
-        jnp.asarray(swap_table(), jnp.bfloat16),
-        jnp.asarray(split_table(), jnp.bfloat16),
-    )
+    )(section, weights, received, swap, split)
     tied = beam.reshape(PER_GROUP, 2, FRAMES, POLS, BEAMS).transpose(0, 1, 3, 2, 4)
     return vis, tied
 
@@ -245,8 +252,14 @@
     inner_h_hbm,
     inner_l_hbm,
     spread_hbm,
+    section_hbm,
+    swap_hbm,
+    split_hbm,
     recv_ref,
-    w_hbm,
+    w_ref,
+    section_ref,
+    swap_ref,
+    split_ref,
     volt_ref,
     band_ref,
     delays_ref,
@@ -257,18 +270,17 @@
     inner_h_ref,
     inner_l_ref,
     spread_ref,
+    choice_ref,
     fh_ref,
     fl_ref,
     y_ref,
     o_ref,
     send_ref,
     pow_ref,
-    w_ref,
     load_sem,
     send_sem,
     recv_sem,
     own_sem,
-    w_sem,
     ready_sem,
 ):
     me, sec = lax.axis_index("stn"), lax.axis_index("sec")
@@ -288,6 +300,9 @@
                 (inner_h_hbm, inner_h_ref),
                 (inner_l_hbm, inner_l_ref),
                 (delays_hbm, delays_ref),
+                (section_hbm, choice_ref),
+                (swap_hbm, swap_ref),
+                (split_hbm, split_ref),
             )
         )
     ]
@@ -300,7 +315,30 @@
     for i in range(1, SECTIONS):
         other = lax.rem(sec + i, SECTIONS)
         pl.semaphore_signal(barrier, inc=1, device_id=(me, other), device_id_type=MESH)
-    for load in loads[:-1]:
+    def greet_later(z, carry):
+        pl.semaphore_signal(
+            barrier, inc=1, device_id=(z * PLANE + place, sec), device_id_type=MESH
+        )
+        return carry
+
+    def greet_earlier(z, carry):
+        pl.semaphore_signal(
+            ready_sem.at[plane], inc=1, device_id=(z * PLANE + place, sec), device_id_type=MESH
+        )
+        return carry
+
+    def meet():
+        pl.semaphore_wait(barrier, PLANE - 1 + SECTIONS - 1 + plane)
+        lax.fori_loop(0, plane, greet_earlier, 0)
+        lax.fori_loop(plane + 1, PLANES, greet_later, 0)
+
+    late = (place // 2 == 4) | (place // 2 == 5)
+
+    @pl.when(late)
+    def _():
+        meet()
+
+    for load in loads[:9]:
         load.wait()
 
     group = lax.broadcasted_iota(jnp.int32, (8, 128), 0)
@@ -381,22 +419,9 @@
     totals = [jnp.sum(p, keepdims=True) for p in powers]
     pow_ref[SECTIONS] = jnp.where(lane < 64, totals[0], totals[1])
 
-    pl.semaphore_wait(barrier, PLANE - 1 + SECTIONS - 1 + plane)
-
-    def greet_later(z, carry):
-        pl.semaphore_signal(
-            barrier, inc=1, device_id=(z * PLANE + place, sec), device_id_type=MESH
-        )
-        return carry
-
-    def greet_earlier(z, carry):
-        pl.semaphore_signal(
-            ready_sem.at[plane], inc=1, device_id=(z * PLANE + place, sec), device_id_type=MESH
-        )
-        return carry
-
-    lax.fori_loop(0, plane, greet_earlier, 0)
-    lax.fori_loop(plane + 1, PLANES, greet_later, 0)
+    @pl.when(jnp.logical_not(late))
+    def _():
+        meet()
 
     def power_copy(j):
         return pltpu.make_async_remote_copy(
@@ -427,15 +452,22 @@
         for i in range(start, PLANE):
             block_copy(z * PLANE + lax.rem(place + i, PLANE), tiles).start()
 
+    high = plane // 4
+    near = plane * (1 - high) + 4 * high
+
     def send_entered(tiles):
-        def one(n, carry):
+        def first(n, carry):
             odd = lax.rem(n, 2)
-            z = (1 - odd) * (n // 2) + odd * (plane - 1 - n // 2)
+            send_plane((1 - odd) * (n // 2) + odd * (near - 1 - n // 2), tiles, 0)
+            return carry
+
+        def then(z, carry):
             send_plane(z, tiles, 0)
             return carry
 
+        lax.fori_loop(0, near, first, 0)
+        lax.fori_loop(near, plane, then, 0)
         send_plane(plane, tiles, 1)
-        lax.fori_loop(0, plane, one, 0)
 
     send_entered(body)
 
@@ -481,22 +513,22 @@
     lax.fori_loop(plane + 1, PLANES, send_later, 0)
     own = pltpu.make_async_copy(send_ref.at[:, me], recv_ref.at[:, me], own_sem)
     own.start()
-    loads[-1].wait()
+    for load in loads[10:]:
+        load.wait()
+    section_ref[...] = jnp.full((8, 128), choice_ref[sec]).astype(jnp.float32)
+    loads[9].wait()
     make_weights(delays_ref[...], sec * NCH + me * PER_GROUP, w_ref)
-    save = pltpu.make_async_copy(w_ref, w_hbm, w_sem)
-    save.start()
     own.wait()
     sent = bytes_of(send_ref.at[:, pl.ds(0, STATIONS - 1)], 1)
     sent.wait_send()
-    save.wait()
     landed = bytes_of(recv_ref.at[:, pl.ds(0, STATIONS - 1)], 1)
     landed.wait_recv()
 
 
-def channelize(flags, volts, band, delays):
+def channelize(volts, band, delays, flags, section):
     outer_h, outer_l = split_const(outer_table())
     inner_h, inner_l = split_const(inner_table())
-    operands = [
+    inputs = [
         volts,
         band,
         delays,
@@ -508,40 +540,53 @@
         jnp.asarray(inner_l),
         jnp.asarray(spread_table(), jnp.bfloat16),
     ]
-    anywhere = pl.BlockSpec(memory_space=pl.ANY)
+    swap = jnp.asarray(swap_table(), jnp.bfloat16)
+    split = jnp.asarray(split_table(), jnp.bfloat16)
+    operands = [
+        pltpu.with_memory_space_constraint(x, pltpu.HBM)
+        for x in inputs + [section, swap, split]
+    ]
+    vmem = pl.BlockSpec(memory_space=pltpu.VMEM)
     return pl.pallas_call(
         channelize_kernel,
         out_shape=(
-            jax.ShapeDtypeStruct((5, STATIONS, POLS, 128), jnp.bfloat16),
-            jax.ShapeDtypeStruct((PER_GROUP, INPUTS, BEAMS), jnp.bfloat16),
+            pltpu.VMEM((5, STATIONS, POLS, 128), jnp.bfloat16),
+            pltpu.VMEM((PER_GROUP, INPUTS, BEAMS), jnp.bfloat16),
+            pltpu.VMEM((8, 128), jnp.float32),
+            pltpu.VMEM(swap.shape, swap.dtype),
+            pltpu.VMEM(split.shape, split.dtype),
         ),
-        in_specs=[pl.BlockSpec(memory_space=pltpu.SMEM)] + [anywhere] * len(operands),
-        out_specs=(anywhere, anywhere),
-        scratch_shapes=[pltpu.VMEM(x.shape, x.dtype) for x in operands]
+        in_specs=[pl.BlockSpec(memory_space=pltpu.SMEM)]
+        + [pl.BlockSpec(memory_space=pltpu.HBM)] * len(operands),
+        out_specs=(vmem,) * 5,
+        scratch_shapes=[pltpu.VMEM(x.shape, x.dtype) for x in inputs]
         + [
+            pltpu.SMEM(section.shape, section.dtype),
             pltpu.VMEM((192, 768), jnp.bfloat16),
             pltpu.VMEM((192, 768), jnp.bfloat16),
             pltpu.VMEM((4, 576, 128), jnp.float32),
             pltpu.VMEM((5, 256, 128), jnp.float32),
             pltpu.VMEM((5, STATIONS, POLS, 128), jnp.bfloat16),
             pltpu.VMEM((5, 1, 128), jnp.float32),
-            pltpu.VMEM((PER_GROUP, INPUTS, BEAMS), jnp.bfloat16),
             pltpu.SemaphoreType.DMA((len(operands),)),
             pltpu.SemaphoreType.DMA((2,)),
             pltpu.SemaphoreType.DMA((2,)),
             pltpu.SemaphoreType.DMA,
-            pltpu.SemaphoreType.DMA,
             pltpu.SemaphoreType.REGULAR((PLANES,)),
         ],
-        compiler_params=pltpu.CompilerParams(collective_id=0, has_side_effects=True),
+        compiler_params=pltpu.CompilerParams(
+            collective_id=0, has_side_effects=True, vmem_limit_bytes=24 << 20
+        ),
         name="channelize",
     )(flags, *operands)
 
 
 def per_device(voltages, bandpass, station_flags, delays, section):
     volts = voltages.reshape(2, POLS, 624, 128).transpose(0, 2, 1, 3).reshape(2, 1248, 128)
-    turned, weights = channelize(station_flags, volts, bandpass, delays)
-    vis, tied = finish(section, weights, turned.reshape(5, INPUTS, 128))
+    turned, weights, choice, swap, split = channelize(
+        volts, bandpass, delays, station_flags, section
+    )
+    vis, tied = finish(choice, weights, turned.reshape(5, INPUTS, 128), swap, split)
     return (vis[None], tied[None])
 
 

time: 34.8 us -> 32.3 us (0.928)
  the two profiles are of different devices: /device:TPU:7 before, /device:TPU:4 now
where the time goes in v1:
time: 32.3 us; the launch traced here: 32.2 us
  Pallas kernels  30.9 us (96%)
  between operations  1.28 us (4%)
    pallas_call x1, Pallas kernels, channelize(): pl.pallas_call(channelize_kernel, out_shape=(pltpu.VMEM((5, STATIONS, POL...  26.7 us
    pallas_call x1, Pallas kernels, finish(): pl.pallas_call(finish_kernel, out_shape=(jax.ShapeDtypeStruct(vis_shape,...  4.15 us

profile of v1, /device:TPU:4, one launch (start us, length us, event | category | flops | bytes accessed | tf_op | source)
XLA Modules:
  0.0 32.2 jit_solution(6809312567022176720)
XLA Ops:
  1.3 26.7 %channelize.1 = (bf16[5,128,2,128]{3,2,1,0:T(2,128)(2,1)S(1)}, bf16[48,256,256]{2,1,0:T(8,128)(2,1)S(1)}, f32[8,128]{1,0:T(8,128)S(1)}, bf16[4,256,256]{2,1,0:T(8,128)(2,1)S(1)}, bf16[256,256]{1,0:T(8,128)(2,1)S(1)}) custom-call(s32[1]{0:T(128)S(6)} %copy.17.flag_ref, bf16[2,1248,128]{2,1,0:T(8,128)(2,1)} %bitcast.13, f32[1,6144]{1,0:T(1,128)} %band_hbm.1, ...), custom_call_target="tpu_custom_call" | custom-call | tf_op jit(solution)/shard_map/channelize/pallas_call | solution.py:550
  28.0 4.1 %finish.1 = (bf16[4,256,256]{2,1,0:T(8,128)(2,1)}, bf16[48,12,2,256]{3,2,1,0:T(2,128)(2,1)}) custom-call(f32[8,128]{1,0:T(8,128)S(1)} %get-tuple-element.9.section_ref, bf16[48,256,256]{2,1,0:T(8,128)(2,1)S(1)} %get-tuple-element.10.w_ref, bf16[5,256,128]{2,1,0:T(8,128)(2,1)S(1)} %bitcast.12, bf16[4,256,256]{2,1,0:T(8,128)(2,1)S(1)} %get-tuple-element.12.swap_ref, ...), custom_call_target="tpu_custom_call" | custom-call | tf_op jit(solution)/shard_map/finish/pallas_call | solution.py:155
